TPU v7x, 256 devices: a whole 4x4x8 slice. The times are simulated.
256 devices in a mesh: rows: 64 (over y, z, core), cols: 4 (over x).
Axes of the slice: x: 4, y: 4, z: 8, core: 2. Of those that a mesh axis runs over, the one named last changes fastest.
Arguments:
- residual_block: float32 [524288, 64], P('rows', 'cols'), may hold values from -6 to 6
- basis: bfloat16 [524288, 64], P('rows', 'cols'), may hold values from -0.0078125 to 0.0078125
- fine_tiles: bfloat16 [4096, 4, 128, 128], P('rows')
- fine_index: int32 [4096, 4], P('rows'), may hold values from 0 to 4095, as said below
- mid_tiles: bfloat16 [512, 3, 128, 128], P('rows')
- fine_owner: int32 [524288], P('rows'), may hold values from 0 to 65535, as said below
- mid_owner: int32 [65536], P('rows'), may hold values from 0 to 8191, as said below
- coarse_inverse: float32 [8192, 8192], P('rows'), as said below
Outputs:
- directions: float32 [524288, 64], P('rows', 'cols')
- gram: float32 [64, 64], P(None, 'cols')
Inputs may be any that keep to these rules, and one draw needn't show every extreme that they name: `fine_index`: slot 0 of block row g names g itself; every block named in a block row of partition p (block rows p*64 to p*64 + 63) belongs to partition p - 1, p or p + 1. `fine_owner`: the fine vertices of partition p map to level-one rows p*1024 to p*1024 + 1023; every level-one row receives exactly 8 vertices. `mid_owner`: the level-one rows of partitions 2q and 2q + 1 map to level-two rows 2q*128 to 2q*128 + 2*128 - 1; every level-two row receives exactly 8 level-one rows. coarse_inverse is symmetric.
All inputs are finite; a program needn't handle non-finite values.
Results may differ from a plain program's by a relative error of at most 0.013.
Values may be sent and summed in bfloat16 or wider, within the bound.
A program may use at most 64 MiB of HBM per device.

v0:
```python
import jax
import jax.numpy as jnp
from jax import lax
from jax.sharding import PartitionSpec as P

DAMPING = 0.6666666666666666


def with_halo(array, sides, width):
    for axis, dim in sides:
        peers, length = (lax.axis_size(axis), array.shape[dim])
        up = [(i, (i + 1) % peers) for i in range(peers - 1)]
        down = [(j, i) for i, j in up]
        last = lax.slice_in_dim(array, length - width, length, axis=dim)
        leading = lax.slice_in_dim(array, 0, width, axis=dim)
        before = lax.ppermute(last, axis, up)
        after = lax.ppermute(leading, axis, down)
        array = jnp.concatenate([before, array, after], axis=dim)
    return array


def swapped(value, axis, apart):
    mask = 2**apart
    pairs = [(source, source ^ mask) for source in range(lax.axis_size(axis))]
    return lax.ppermute(value, axis, pairs)


def fine_apply(vector, matrix, window_index):
    extent = matrix.shape[2]
    packed = vector.astype(jnp.bfloat16).reshape(-1, extent, vector.shape[1])
    window = with_halo(packed, (("rows", 0),), packed.shape[0])
    picked = window[window_index]
    product = jnp.einsum("bkij,bkjc->bic", matrix, picked, preferred_element_type=jnp.float32)
    return product.reshape(vector.shape)


def mid_apply(vector, matrix):
    blocks = matrix.shape[0]
    extent = matrix.shape[2]
    packed = vector.astype(jnp.bfloat16).reshape(blocks, extent, vector.shape[1])
    window = with_halo(packed, (("rows", 0),), 1)
    product = jnp.einsum(
        "bij,bjc->bic", matrix[:, 0], window[:-2], preferred_element_type=jnp.float32
    )
    product = product + jnp.einsum(
        "bij,bjc->bic", matrix[:, 1], window[1:-1], preferred_element_type=jnp.float32
    )
    product = product + jnp.einsum(
        "bij,bjc->bic", matrix[:, 2], window[2:], preferred_element_type=jnp.float32
    )
    return product.reshape(vector.shape)


def on_device(
    residual_block, basis, fine_tiles, fine_index, mid_tiles, fine_owner, mid_owner, coarse_inverse
):
    device = lax.axis_index("rows")
    blocks = fine_tiles.shape[0]
    mid_count = mid_tiles.shape[0] * mid_tiles.shape[2]
    coarse_count = coarse_inverse.shape[0]
    col_width = residual_block.shape[1]
    parity = device % 2
    window_index = fine_index - (device - 1) * blocks
    fine_local = fine_owner - device * mid_count
    mid_local = mid_owner - (device - parity) * coarse_count
    fine_inv = 1.0 / jnp.diagonal(fine_tiles[:, 0], axis1=1, axis2=2).astype(jnp.float32).reshape(
        -1, 1
    )
    mid_inv = 1.0 / jnp.diagonal(mid_tiles[:, 1], axis1=1, axis2=2).astype(jnp.float32).reshape(
        -1, 1
    )
    fine_x = DAMPING * fine_inv * residual_block
    fine_x = fine_x + DAMPING * fine_inv * (
        residual_block - fine_apply(fine_x, fine_tiles, window_index)
    )
    fine_res = residual_block - fine_apply(fine_x, fine_tiles, window_index)
    partial_mid = jax.ops.segment_sum(fine_res, fine_local, num_segments=mid_count)
    mid_x = DAMPING * mid_inv * partial_mid
    mid_x = mid_x + DAMPING * mid_inv * (partial_mid - mid_apply(mid_x, mid_tiles))
    mid_res = partial_mid - mid_apply(mid_x, mid_tiles)
    partial_value = jax.ops.segment_sum(mid_res, mid_local, num_segments=2 * coarse_count)
    halves = partial_value.reshape(2, coarse_count, col_width)
    own_half = jnp.where(parity == 0, halves[0], halves[1])
    other_half = jnp.where(parity == 0, halves[1], halves[0])
    coarse_rhs = own_half + swapped(other_half, "rows", 0)
    coarse_fix = jnp.dot(
        coarse_inverse,
        lax.all_gather(coarse_rhs, "rows", axis=0, tiled=True),
        precision=lax.Precision.HIGHEST,
        preferred_element_type=jnp.float32,
    )
    partner_fix = swapped(coarse_fix, "rows", 0)
    pair_values = jnp.where(
        parity == 0,
        jnp.concatenate([coarse_fix, partner_fix], axis=0),
        jnp.concatenate([partner_fix, coarse_fix], axis=0),
    )
    mid_x = mid_x + pair_values[mid_local]
    mid_x = mid_x + DAMPING * mid_inv * (partial_mid - mid_apply(mid_x, mid_tiles))
    fine_x = fine_x + mid_x[fine_local]
    finished = fine_x + DAMPING * fine_inv * (
        residual_block - fine_apply(fine_x, fine_tiles, window_index)
    )
    rounded = finished.astype(jnp.bfloat16)
    partial_gram = lax.dot_general(
        lax.all_gather(basis, "cols", axis=1, tiled=True),
        rounded,
        (((0,), (0,)), ((), ())),
        preferred_element_type=jnp.float32,
    )
    gram = lax.psum(partial_gram, "rows")
    return (finished, gram)


def solution(mesh):
    in_specs = (
        P("rows", "cols"),
        P("rows", "cols"),
        P("rows", None, None, None),
        P("rows", None),
        P("rows", None, None, None),
        P("rows"),
        P("rows"),
        P("rows", None),
    )
    out_specs = (P("rows", "cols"), P(None, "cols"))
    return jax.shard_map(
        on_device, mesh=mesh, in_specs=in_specs, out_specs=out_specs, check_vma=False
    )
```

profile of v0, /device:TPU:4, one launch (start us, length us, event | category | flops | bytes accessed | tf_op | source)
XLA Modules:
  0.0 407.9 jit_solution(2754003155523653004)
XLA Ops:
  7.2 1.5 slice-done
  8.8 3.9 copy.204
  12.7 1.9 gather_fusion
  14.8 1.8 collective-permute-start
  16.5 1.3 collective-permute-start.1
  19.1 3.1 copy.166
  22.2 1.9 gather_fusion.2
  25.2 5.7 %convolution_bitcast_fusion.2 = f32[64,2,8,128]{3,2,1,0:T(8,128)S(1)} fusion(bf16[64,4,128,16]{2,3,1,0:T(8,128)(2,1)S(1)} %bitcast.177, bf16[64,4,128,128]{3,2,1,0:T(8,128)(2,1)} %param.10), kind=kOutput, calls=%fused_computation.11 | convolution fusion | flops 134217728 | bytes 9961472 | tf_op jit(solution)/shard_map/bkij,bkjc->bic/dot_general | solution.py:33
  31.0 4.7 %collective-permute-start.2 = (bf16[64,128,16]{1,2,0:T(8,128)(2,1)S(1)}, bf16[64,128,16]{1,2,0:T(8,128)(2,1)S(1)}, u32[]{:S(2)}, u32[]{:S(2)}) collective-permute-start(bf16[64,128,16]{1,2,0:T(8,128)(2,1)S(1)} %copy_bitcast_fusion.1), channel_id=1, source_target_pairs={{0,4},{4,8},{8,12},{12,16},{16,20},{20,24},{24,28},{28,32},{32,36}... | collective-permute-start | bytes 786440 | tf_op jit(solution)/shard_map/ppermute | solution.py:16
  37.1 3.3 collective-permute-done.3
  41.3 5.7 %convolution_bitcast_fusion.1 = f32[64,2,8,128]{3,2,1,0:T(8,128)S(1)} fusion(bf16[64,4,128,16]{2,3,1,0:T(8,128)(2,1)S(1)} %bitcast.178, bf16[64,4,128,128]{3,2,1,0:T(8,128)(2,1)} %param.10), kind=kOutput, calls=%fused_computation.10 | convolution fusion | flops 134217728 | bytes 9961472 | tf_op jit(solution)/shard_map/bkij,bkjc->bic/dot_general | solution.py:33
  47.1 2.6 copy.172
  49.7 44.4 %scatter_custom_fusion = f32[1024,16]{1,0:T(8,128)S(1)} fusion(s32[8192]{0:T(1024)S(1)} %get-tuple-element.11, f32[8192,16]{1,0:T(8,128)} %copy.172, f32[]{:T(128)} %constant.25.clone.1), kind=kCustom, calls=%fused_computation.51 | custom fusion | flops 131072 | bytes 66048 | tf_op jit(solution)/shard_map/scatter-add | solution.py:77
  94.6 1.3 collective-permute-start.5
  95.9 7.3 %collective-permute-start.4 = (bf16[1,128,16]{1,2,0:T(8,128)(2,1)S(1)}, bf16[1,128,16]{1,2,0:T(8,128)(2,1)S(1)}, u32[]{:S(2)}, u32[]{:S(2)}) collective-permute-start(bf16[1,128,16]{1,2,0:T(8,128)(2,1)S(1)} %get-tuple-element.18), channel_id=1, source_target_pairs={{0,4},{4,8},{8,12},{12,16},{16,20},{20,24},{24,28},{28,32},{32,36}... | collective-permute-start | bytes 12296 | tf_op jit(solution)/shard_map/ppermute | solution.py:16
  104.5 1.3 collective-permute-start.7
  105.8 4.2 %collective-permute-start.6 = (bf16[1,128,16]{1,2,0:T(8,128)(2,1)S(1)}, bf16[1,128,16]{1,2,0:T(8,128)(2,1)S(1)}, u32[]{:S(2)}, u32[]{:S(2)}) collective-permute-start(bf16[1,128,16]{1,2,0:T(8,128)(2,1)S(1)} %get-tuple-element.16), channel_id=1, source_target_pairs={{0,4},{4,8},{8,12},{12,16},{16,20},{20,24},{24,28},{28,32},{32,36}... | collective-permute-start | bytes 12296 | tf_op jit(solution)/shard_map/ppermute | solution.py:16
  112.2 6.4 %scatter_custom_fusion.1 = f32[256,16]{1,0:T(8,128)S(1)} fusion(s32[1024]{0:T(1024)S(1)} %get-tuple-element.13, f32[1024,16]{1,0:T(8,128)} %bitcast_subtract_fusion.3, f32[]{:T(128)} %constant.25.clone.1), kind=kCustom, calls=%fused_computation.70 | custom fusion | flops 16384 | bytes 16896 | tf_op jit(solution)/shard_map/scatter-add | solution.py:81
  118.6 2.5 collective-permute-start.8
  122.0 65.2 %all_gather.6 = f32[8192,16]{1,0:T(8,128)S(1)} all-gather(f32[128,16]{1,0:T(8,128)S(1)} %select_add_fusion), channel_id=1, replica_groups=mesh['rows'=64,'cols'=4] {'rows'}, dimensions={0}, use_global_device_ids=true | all-gather | bytes 532480 | tf_op jit(solution)/shard_map/all_gather | solution.py:88
  187.2 6.6 %convolution_bitcast_fusion.4 = f32[128,16]{0,1:T(8,128)S(1)} fusion(f32[8192,16]{1,0:T(8,128)S(1)} %all_gather.6, f32[128,8192]{1,0:T(8,128)S(1)} %copy-done.2), kind=kOutput, calls=%fused_computation.22 | convolution fusion | flops 201326592 | bytes 4726784 | tf_op jit(solution)/shard_map/dot_general | solution.py:86
  195.1 2.8 gather_fusion.4
  198.4 1.3 collective-permute-start.11
  199.7 3.0 collective-permute-start.10
  204.0 27.9 %gather_fusion.5 = f32[8192,16]{1,0:T(8,128)} fusion(f32[1024,16]{1,0:T(8,128)S(1)} %copy.193, s32[8192]{0:T(1024)S(1)} %get-tuple-element.10), kind=kCustom, calls=%fused_computation.5 | custom fusion | bytes 1081344 | tf_op jit(solution)/shard_map/gather | solution.py:100
  231.9 2.8 copy.194
  234.8 3.4 collective-permute-start.12
  239.6 3.9 collective-permute-done.13
  244.4 5.7 %convolution_bitcast_fusion = f32[64,2,8,128]{3,2,1,0:T(8,128)S(1)} fusion(bf16[64,4,128,16]{2,3,1,0:T(8,128)(2,1)S(1)} %bitcast.176, bf16[64,4,128,128]{3,2,1,0:T(8,128)(2,1)} %param.10), kind=kOutput, calls=%fused_computation.9 | convolution fusion | flops 134217728 | bytes 9961472 | tf_op jit(solution)/shard_map/bkij,bkjc->bic/dot_general | solution.py:33
  250.3 18.4 %all-gather.2.cloned.1.call-done = bf16[8192,64]{0,1:T(8,128)(2,1)} async-done(((bf16[8192,16]{0,1:T(8,128)(2,1)}), bf16[8192,64]{0,1:T(8,128)(2,1)}) %all-gather.2.cloned.1.call-update) | async-done | bytes 1048592 | tf_op jit(solution)/shard_map/all_gather | solution.py:106
  268.7 1.6 convolution_bitcast_fusion.3
  270.3 130.8 %psum.7 = f32[64,16]{0,1:T(8,128)} all-reduce(f32[64,16]{0,1:T(8,128)S(1)} %convolution_bitcast_fusion.3), channel_id=1, replica_groups=mesh['rows'=64,'cols'=4] {'rows'}, use_global_device_ids=true, to_apply=%region_2.3 | all-reduce | flops 1024 | bytes 8192 | tf_op jit(solution)/shard_map/psum | solution.py:111
  (83 shorter events, 15.2 us)
Async XLA Ops:
  7.2 1.6 slice-start
  7.2 261.5 %all-gather.2.cloned.1.call-start = ((), (), s32[]{:S(2)}) async-start(), calls=%async_computation | async-start | bytes 1310720 | tf_op jit(solution)/shard_map/all_gather | solution.py:106
  8.8 6.0 %copy-start = (f32[8192,16]{0,1:T(8,128)S(1)}, f32[8192,16]{0,1:T(8,128)}, u32[]{:S(2)}) copy-start(f32[8192,16]{0,1:T(8,128)} %param.8) | copy-start | bytes 1572868
  8.8 9.1 %copy-start.6 = (s32[64,4]{0,1:T(4,128)S(1)}, s32[64,4]{0,1:T(4,128)}, u32[]{:S(2)}) copy-start(s32[64,4]{0,1:T(4,128)} %param.11) | copy-start | bytes 3076
  12.7 11.5 %copy-start.5 = (s32[1024]{0:T(1024)S(1)}, s32[1024]{0:T(1024)}, u32[]{:S(2)}) copy-start(s32[1024]{0:T(1024)} %param.14) | copy-start | bytes 12292
  14.8 9.4 %collective-permute-start = (bf16[64,128,16]{1,2,0:T(8,128)(2,1)S(1)}, bf16[64,128,16]{1,2,0:T(8,128)(2,1)S(1)}, u32[]{:S(2)}, u32[]{:S(2)}) collective-permute-start(bf16[64,128,16]{1,2,0:T(8,128)(2,1)S(1)} %copy_bitcast_fusion.2), channel_id=1, source_target_pairs={{0,4},{4,8},{8,12},{12,16},{16,20},{20,24},{24,28},{28,32},{32,36}... | collective-permute-start | bytes 786440 | tf_op jit(solution)/shard_map/ppermute | solution.py:16
  16.5 7.7 %collective-permute-start.1 = (bf16[64,128,16]{1,2,0:T(8,128)(2,1)S(1)}, bf16[64,128,16]{1,2,0:T(8,128)(2,1)S(1)}, u32[]{:S(2)}, u32[]{:S(2)}) collective-permute-start(bf16[64,128,16]{1,2,0:T(8,128)(2,1)S(1)} %copy_bitcast_fusion.2), channel_id=1, source_target_pairs={{4,0},{8,4},{12,8},{16,12},{20,16},{24,20},{28,24},{32,28},{36,32}... | collective-permute-start | bytes 786440 | tf_op jit(solution)/shard_map/ppermute | solution.py:17
  25.2 11.9 %copy-start.4 = (s32[8192]{0:T(1024)S(1)}, s32[8192]{0:T(1024)}, u32[]{:S(2)}) copy-start(s32[8192]{0:T(1024)} %param.13) | copy-start | bytes 98308
  31.0 6.1 %collective-permute-start.2 = (bf16[64,128,16]{1,2,0:T(8,128)(2,1)S(1)}, bf16[64,128,16]{1,2,0:T(8,128)(2,1)S(1)}, u32[]{:S(2)}, u32[]{:S(2)}) collective-permute-start(bf16[64,128,16]{1,2,0:T(8,128)(2,1)S(1)} %copy_bitcast_fusion.1), channel_id=1, source_target_pairs={{0,4},{4,8},{8,12},{12,16},{16,20},{20,24},{24,28},{28,32},{32,36}... | collective-permute-start | bytes 786440 | tf_op jit(solution)/shard_map/ppermute | solution.py:16
  35.7 4.7 %collective-permute-start.3 = (bf16[64,128,16]{1,2,0:T(8,128)(2,1)S(1)}, bf16[64,128,16]{1,2,0:T(8,128)(2,1)S(1)}, u32[]{:S(2)}, u32[]{:S(2)}) collective-permute-start(bf16[64,128,16]{1,2,0:T(8,128)(2,1)S(1)} %copy_bitcast_fusion.1), channel_id=1, source_target_pairs={{4,0},{8,4},{12,8},{16,12},{20,16},{24,20},{28,24},{32,28},{36,32}... | collective-permute-start | bytes 786440 | tf_op jit(solution)/shard_map/ppermute | solution.py:17
  47.0 47.3 %copy-start.1 = (bf16[8,3,128,128]{3,2,1,0:T(8,128)(2,1)S(1)}, bf16[8,3,128,128]{3,2,1,0:T(8,128)(2,1)}, u32[]{:S(2)}) copy-start(bf16[8,3,128,128]{3,2,1,0:T(8,128)(2,1)} %param.12) | copy-start | bytes 2359300
  94.6 8.6 %collective-permute-start.5 = (bf16[1,128,16]{1,2,0:T(8,128)(2,1)S(1)}, bf16[1,128,16]{1,2,0:T(8,128)(2,1)S(1)}, u32[]{:S(2)}, u32[]{:S(2)}) collective-permute-start(bf16[1,128,16]{1,2,0:T(8,128)(2,1)S(1)} %get-tuple-element.19), channel_id=1, source_target_pairs={{4,0},{8,4},{12,8},{16,12},{20,16},{24,20},{28,24},{32,28},{36,32}... | collective-permute-start | bytes 12296 | tf_op jit(solution)/shard_map/ppermute | solution.py:17
  95.9 8.1 %collective-permute-start.4 = (bf16[1,128,16]{1,2,0:T(8,128)(2,1)S(1)}, bf16[1,128,16]{1,2,0:T(8,128)(2,1)S(1)}, u32[]{:S(2)}, u32[]{:S(2)}) collective-permute-start(bf16[1,128,16]{1,2,0:T(8,128)(2,1)S(1)} %get-tuple-element.18), channel_id=1, source_target_pairs={{0,4},{4,8},{8,12},{12,16},{16,20},{20,24},{24,28},{28,32},{32,36}... | collective-permute-start | bytes 12296 | tf_op jit(solution)/shard_map/ppermute | solution.py:16
  104.5 5.5 %collective-permute-start.7 = (bf16[1,128,16]{1,2,0:T(8,128)(2,1)S(1)}, bf16[1,128,16]{1,2,0:T(8,128)(2,1)S(1)}, u32[]{:S(2)}, u32[]{:S(2)}) collective-permute-start(bf16[1,128,16]{1,2,0:T(8,128)(2,1)S(1)} %get-tuple-element.17), channel_id=1, source_target_pairs={{4,0},{8,4},{12,8},{16,12},{20,16},{24,20},{28,24},{32,28},{36,32}... | collective-permute-start | bytes 12296 | tf_op jit(solution)/shard_map/ppermute | solution.py:17
  105.8 5.0 %collective-permute-start.6 = (bf16[1,128,16]{1,2,0:T(8,128)(2,1)S(1)}, bf16[1,128,16]{1,2,0:T(8,128)(2,1)S(1)}, u32[]{:S(2)}, u32[]{:S(2)}) collective-permute-start(bf16[1,128,16]{1,2,0:T(8,128)(2,1)S(1)} %get-tuple-element.16), channel_id=1, source_target_pairs={{0,4},{4,8},{8,12},{12,16},{16,20},{20,24},{24,28},{28,32},{32,36}... | collective-permute-start | bytes 12296 | tf_op jit(solution)/shard_map/ppermute | solution.py:16
  118.6 68.6 %copy-start.2 = (f32[128,8192]{1,0:T(8,128)S(1)}, f32[128,8192]{1,0:T(8,128)}, u32[]{:S(2)}) copy-start(f32[128,8192]{1,0:T(8,128)} %param.15) | copy-start | bytes 12582916
  118.6 3.4 collective-permute-start.8
  193.8 1.2 collective-permute-start.9
  198.4 4.4 %collective-permute-start.11 = (bf16[1,128,16]{1,2,0:T(8,128)(2,1)S(1)}, bf16[1,128,16]{1,2,0:T(8,128)(2,1)S(1)}, u32[]{:S(2)}, u32[]{:S(2)}) collective-permute-start(bf16[1,128,16]{1,2,0:T(8,128)(2,1)S(1)} %get-tuple-element.15), channel_id=1, source_target_pairs={{4,0},{8,4},{12,8},{16,12},{20,16},{24,20},{28,24},{32,28},{36,32}... | collective-permute-start | bytes 12296 | tf_op jit(solution)/shard_map/ppermute | solution.py:17
  199.7 3.8 collective-permute-start.10
  234.8 4.8 %collective-permute-start.12 = (bf16[64,128,16]{1,2,0:T(8,128)(2,1)S(1)}, bf16[64,128,16]{1,2,0:T(8,128)(2,1)S(1)}, u32[]{:S(2)}, u32[]{:S(2)}) collective-permute-start(bf16[64,128,16]{1,2,0:T(8,128)(2,1)S(1)} %copy_bitcast_fusion), channel_id=1, source_target_pairs={{0,4},{4,8},{8,12},{12,16},{16,20},{20,24},{24,28},{28,32},{32,36}... | collective-permute-start | bytes 786440 | tf_op jit(solution)/shard_map/ppermute | solution.py:16
  238.3 5.2 %collective-permute-start.13 = (bf16[64,128,16]{1,2,0:T(8,128)(2,1)S(1)}, bf16[64,128,16]{1,2,0:T(8,128)(2,1)S(1)}, u32[]{:S(2)}, u32[]{:S(2)}) collective-permute-start(bf16[64,128,16]{1,2,0:T(8,128)(2,1)S(1)} %copy_bitcast_fusion), channel_id=1, source_target_pairs={{4,0},{8,4},{12,8},{16,12},{20,16},{24,20},{28,24},{32,28},{36,32}... | collective-permute-start | bytes 786440 | tf_op jit(solution)/shard_map/ppermute | solution.py:17
  250.3 150.8 %copy-start.3 = (f32[8192,16]{0,1:T(8,128)}, f32[8192,16]{0,1:T(8,128)S(1)}, u32[]{:S(2)}) copy-start(f32[8192,16]{0,1:T(8,128)S(1)} %fusion.7) | copy-start | bytes 1572868
Sparse Core Ops, SparseCore 0:
  239.7 28.9 all-gather.1
where the time goes:
time: 409 us; the launch traced here: 408 us
  blocking collectives  196 us (48%)
  local copies, waits for them, and re-layouts  53.3 us (13%)
  other arithmetic  52.8 us (13%)
  starting transfers between devices  35.1 us (9%)
  waiting for transfers between devices  29 us (7%)
  matrix products  27.3 us (7%)
  between operations  14.5 us (4%)
    psum x1, blocking collectives, on_device(): gram = lax.psum(partial_gram, 'rows')  131 us
    all_gather x1, blocking collectives, on_device(): lax.all_gather(coarse_rhs, 'rows', axis=0, tiled=True)  65.2 us
    scatter-add x1, other arithmetic, on_device(): jax.ops.segment_sum(fine_res, fine_local, num_segments=mid_count)  44.4 us
    gather x2, local copies, waits for them, and re-layouts, on_device(): fine_x = fine_x + mid_x[fine_local]  30.7 us
    ppermute x6, starting transfers between devices, with_halo(): before = lax.ppermute(last, axis, up)  24.4 us
    all_gather x1, waiting for transfers between devices, on_device(): lax.all_gather(basis, 'cols', axis=1, tiled=True)  18.4 us
    dot_general x3, matrix products, fine_apply(): jnp.einsum('bkij,bkjc->bic', matrix, picked, preferred_element_type=jnp.f...  17 us
  transfers between devices with their start and end apart: 15, of which 8 were waited for; matrix products, arithmetic and copies ran while one was open for 3% of the time, Pallas kernels for 0%

commit v1 on v0

--- a/solution.py
+++ b/solution.py
@@ -108,7 +108,8 @@
         (((0,), (0,)), ((), ())),
         preferred_element_type=jnp.float32,
     )
-    gram = lax.psum(partial_gram, "rows")
+    parts = lax.all_gather(partial_gram, "rows")
+    gram = jnp.sum(parts, axis=0)
     return (finished, gram)
 
 

time: 409 us -> 332 us (0.81)
  blocking collectives: 196 us -> 116 us
    psum x1 -> x0, blocking collectives: 131 us -> none  [on_device(): gram = lax.psum(partial_gram, 'rows')]
    all_gather x0 -> x1, blocking collectives: none -> 51.1 us  [on_device(): parts = lax.all_gather(partial_gram, 'rows')]
  transfers between devices with their start and end apart: 15 -> 15, of which waited for: 8 -> 8; matrix products, arithmetic and copies ran while one was open for 3% -> 4% of each run, Pallas kernels for 0% -> 0%
where the time goes in v1:
time: 332 us; the launch traced here: 329 us
  blocking collectives  116 us (35%)
  other arithmetic  53.5 us (16%)
  local copies, waits for them, and re-layouts  53.3 us (16%)
  starting transfers between devices  35.3 us (11%)
  waiting for transfers between devices  29 us (9%)
  matrix products  27.3 us (8%)
  between operations  14.5 us (4%)
    all_gather x1, blocking collectives, on_device(): lax.all_gather(coarse_rhs, 'rows', axis=0, tiled=True)  65.2 us
    all_gather x1, blocking collectives, on_device(): parts = lax.all_gather(partial_gram, 'rows')  51.1 us
    scatter-add x1, other arithmetic, on_device(): jax.ops.segment_sum(fine_res, fine_local, num_segments=mid_count)  44.4 us
    gather x2, local copies, waits for them, and re-layouts, on_device(): fine_x = fine_x + mid_x[fine_local]  30.7 us
    ppermute x6, starting transfers between devices, with_halo(): before = lax.ppermute(last, axis, up)  24.4 us
    all_gather x1, waiting for transfers between devices, on_device(): lax.all_gather(basis, 'cols', axis=1, tiled=True)  18.6 us
    dot_general x3, matrix products, fine_apply(): jnp.einsum('bkij,bkjc->bic', matrix, picked, preferred_element_type=jnp.f...  17 us
    ppermute x6, starting transfers between devices, with_halo(): after = lax.ppermute(leading, axis, down)  8 us
  transfers between devices with their start and end apart: 15, of which 8 were waited for; matrix products, arithmetic and copies ran while one was open for 4% of the time, Pallas kernels for 0%

profile of v1, /device:TPU:4, one launch (start us, length us, event | category | flops | bytes accessed | tf_op | source)
XLA Modules:
  0.0 329.1 jit_solution(10381056839730479344)
XLA Ops:
  7.2 1.5 slice-done
  8.8 3.9 %copy.204 = bf16[64,1,128,128]{0,3,2,1:T(8,128)(2,1)} copy(bf16[64,1,128,128]{3,2,1,0:T(8,128)(2,1)S(1)} %slice-done) | data formatting | bytes 4194304
  12.7 1.9 gather_fusion
  14.8 1.8 collective-permute-start
  19.1 3.1 copy.166
  22.2 1.9 gather_fusion.2
  25.2 5.7 %convolution_bitcast_fusion.2 = f32[64,2,8,128]{3,2,1,0:T(8,128)S(1)} fusion(bf16[64,4,128,16]{2,3,1,0:T(8,128)(2,1)S(1)} %bitcast.179, bf16[64,4,128,128]{3,2,1,0:T(8,128)(2,1)} %param.10), kind=kOutput, calls=%fused_computation.11 | convolution fusion | flops 134217728 | bytes 9961472 | tf_op jit(solution)/shard_map/bkij,bkjc->bic/dot_general | solution.py:33
  31.0 4.7 %collective-permute-start.2 = (bf16[64,128,16]{1,2,0:T(8,128)(2,1)S(1)}, bf16[64,128,16]{1,2,0:T(8,128)(2,1)S(1)}, u32[]{:S(2)}, u32[]{:S(2)}) collective-permute-start(bf16[64,128,16]{1,2,0:T(8,128)(2,1)S(1)} %copy_bitcast_fusion.1), channel_id=1, source_target_pairs={{0,4},{4,8},{8,12},{12,16},{16,20},{20,24},{24,28},{28,32},{32,36}... | collective-permute-start | bytes 786440 | tf_op jit(solution)/shard_map/ppermute | solution.py:16
  37.1 3.3 %collective-permute-done.3 = bf16[64,128,16]{1,2,0:T(8,128)(2,1)S(1)} collective-permute-done((bf16[64,128,16]{1,2,0:T(8,128)(2,1)S(1)}, bf16[64,128,16]{1,2,0:T(8,128)(2,1)S(1)}, u32[]{:S(2)}, u32[]{:S(2)}) %collective-permute-start.3) | collective-permute-done | bytes 262176 | tf_op jit(solution)/shard_map/ppermute | solution.py:17
  41.3 5.7 %convolution_bitcast_fusion.1 = f32[64,2,8,128]{3,2,1,0:T(8,128)S(1)} fusion(bf16[64,4,128,16]{2,3,1,0:T(8,128)(2,1)S(1)} %bitcast.180, bf16[64,4,128,128]{3,2,1,0:T(8,128)(2,1)} %param.10), kind=kOutput, calls=%fused_computation.10 | convolution fusion | flops 134217728 | bytes 9961472 | tf_op jit(solution)/shard_map/bkij,bkjc->bic/dot_general | solution.py:33
  47.1 2.6 copy.172
  49.7 44.4 %scatter_custom_fusion = f32[1024,16]{1,0:T(8,128)S(1)} fusion(s32[8192]{0:T(1024)S(1)} %get-tuple-element.11, f32[8192,16]{1,0:T(8,128)} %copy.172, f32[]{:T(128)} %constant.25.clone.1), kind=kCustom, calls=%fused_computation.51 | custom fusion | flops 131072 | bytes 66048 | tf_op jit(solution)/shard_map/scatter-add | solution.py:77
  94.6 1.3 collective-permute-start.5
  95.9 7.3 %collective-permute-start.4 = (bf16[1,128,16]{1,2,0:T(8,128)(2,1)S(1)}, bf16[1,128,16]{1,2,0:T(8,128)(2,1)S(1)}, u32[]{:S(2)}, u32[]{:S(2)}) collective-permute-start(bf16[1,128,16]{1,2,0:T(8,128)(2,1)S(1)} %get-tuple-element.18), channel_id=1, source_target_pairs={{0,4},{4,8},{8,12},{12,16},{16,20},{20,24},{24,28},{28,32},{32,36}... | collective-permute-start | bytes 12296 | tf_op jit(solution)/shard_map/ppermute | solution.py:16
  104.5 1.3 collective-permute-start.7
  105.8 4.2 %collective-permute-start.6 = (bf16[1,128,16]{1,2,0:T(8,128)(2,1)S(1)}, bf16[1,128,16]{1,2,0:T(8,128)(2,1)S(1)}, u32[]{:S(2)}, u32[]{:S(2)}) collective-permute-start(bf16[1,128,16]{1,2,0:T(8,128)(2,1)S(1)} %get-tuple-element.16), channel_id=1, source_target_pairs={{0,4},{4,8},{8,12},{12,16},{16,20},{20,24},{24,28},{28,32},{32,36}... | collective-permute-start | bytes 12296 | tf_op jit(solution)/shard_map/ppermute | solution.py:16
  112.2 6.4 %scatter_custom_fusion.1 = f32[256,16]{1,0:T(8,128)S(1)} fusion(s32[1024]{0:T(1024)S(1)} %get-tuple-element.13, f32[1024,16]{1,0:T(8,128)} %bitcast_subtract_fusion.3, f32[]{:T(128)} %constant.25.clone.1), kind=kCustom, calls=%fused_computation.70 | custom fusion | flops 16384 | bytes 16896 | tf_op jit(solution)/shard_map/scatter-add | solution.py:81
  118.6 2.5 collective-permute-start.8
  122.0 65.2 %all_gather.12 = f32[8192,16]{1,0:T(8,128)S(1)} all-gather(f32[128,16]{1,0:T(8,128)S(1)} %select_add_fusion), channel_id=1, replica_groups=mesh['rows'=64,'cols'=4] {'rows'}, dimensions={0}, use_global_device_ids=true | all-gather | bytes 532480 | tf_op jit(solution)/shard_map/all_gather | solution.py:88
  187.2 6.6 %convolution_bitcast_fusion.4 = f32[128,16]{0,1:T(8,128)S(1)} fusion(f32[8192,16]{1,0:T(8,128)S(1)} %all_gather.12, f32[128,8192]{1,0:T(8,128)S(1)} %copy-done.2), kind=kOutput, calls=%fused_computation.22 | convolution fusion | flops 201326592 | bytes 4726784 | tf_op jit(solution)/shard_map/dot_general | solution.py:86
  195.1 2.8 gather_fusion.4
  198.4 1.3 collective-permute-start.11
  199.7 3.0 collective-permute-start.10
  204.0 27.9 %gather_fusion.5 = f32[8192,16]{1,0:T(8,128)} fusion(f32[1024,16]{1,0:T(8,128)S(1)} %copy.193, s32[8192]{0:T(1024)S(1)} %get-tuple-element.10), kind=kCustom, calls=%fused_computation.5 | custom fusion | bytes 1081344 | tf_op jit(solution)/shard_map/gather | solution.py:100
  231.9 2.8 copy.194
  234.8 3.4 %collective-permute-start.12 = (bf16[64,128,16]{1,2,0:T(8,128)(2,1)S(1)}, bf16[64,128,16]{1,2,0:T(8,128)(2,1)S(1)}, u32[]{:S(2)}, u32[]{:S(2)}) collective-permute-start(bf16[64,128,16]{1,2,0:T(8,128)(2,1)S(1)} %copy_bitcast_fusion), channel_id=1, source_target_pairs={{0,4},{4,8},{8,12},{12,16},{16,20},{20,24},{24,28},{28,32},{32,36}... | collective-permute-start | bytes 786440 | tf_op jit(solution)/shard_map/ppermute | solution.py:16
  238.3 1.5 collective-permute-start.13
  239.8 3.6 %collective-permute-done.13 = bf16[64,128,16]{1,2,0:T(8,128)(2,1)S(1)} collective-permute-done((bf16[64,128,16]{1,2,0:T(8,128)(2,1)S(1)}, bf16[64,128,16]{1,2,0:T(8,128)(2,1)S(1)}, u32[]{:S(2)}, u32[]{:S(2)}) %collective-permute-start.13) | collective-permute-done | bytes 262176 | tf_op jit(solution)/shard_map/ppermute | solution.py:17
  244.4 5.7 %convolution_bitcast_fusion = f32[64,2,8,128]{3,2,1,0:T(8,128)S(1)} fusion(bf16[64,4,128,16]{2,3,1,0:T(8,128)(2,1)S(1)} %bitcast.178, bf16[64,4,128,128]{3,2,1,0:T(8,128)(2,1)} %param.10), kind=kOutput, calls=%fused_computation.9 | convolution fusion | flops 134217728 | bytes 9961472 | tf_op jit(solution)/shard_map/bkij,bkjc->bic/dot_general | solution.py:33
  250.3 18.6 %all-gather.4.cloned.1.call-done = bf16[8192,64]{0,1:T(8,128)(2,1)} async-done(((bf16[8192,16]{0,1:T(8,128)(2,1)}), bf16[8192,64]{0,1:T(8,128)(2,1)}) %all-gather.4.cloned.1.call-update) | async-done | bytes 1048592 | tf_op jit(solution)/shard_map/all_gather | solution.py:106
  268.9 1.6 convolution_bitcast_fusion.3
  270.5 51.1 %all-gather.1 = f32[64,64,16]{1,2,0:T(8,128)S(1)} all-gather(f32[1,64,16]{1,2,0:T(8,128)S(1)} %convolution_bitcast_fusion.3), channel_id=2, replica_groups=mesh['rows'=64,'cols'=4] {'rows'}, dimensions={0}, use_global_device_ids=true | all-gather | bytes 266240 | tf_op jit(solution)/shard_map/all_gather | solution.py:111
  (84 shorter events, 15.9 us)
Async XLA Ops:
  7.2 1.6 slice-start
  7.2 261.7 %all-gather.4.cloned.1.call-start = ((), (), s32[]{:S(2)}) async-start(), calls=%async_computation | async-start | bytes 1310720 | tf_op jit(solution)/shard_map/all_gather | solution.py:106
  8.8 6.0 %copy-start = (f32[8192,16]{0,1:T(8,128)S(1)}, f32[8192,16]{0,1:T(8,128)}, u32[]{:S(2)}) copy-start(f32[8192,16]{0,1:T(8,128)} %param.8) | copy-start | bytes 1572868
  8.8 9.1 %copy-start.6 = (s32[64,4]{0,1:T(4,128)S(1)}, s32[64,4]{0,1:T(4,128)}, u32[]{:S(2)}) copy-start(s32[64,4]{0,1:T(4,128)} %param.11) | copy-start | bytes 3076
  12.7 11.5 %copy-start.5 = (s32[1024]{0:T(1024)S(1)}, s32[1024]{0:T(1024)}, u32[]{:S(2)}) copy-start(s32[1024]{0:T(1024)} %param.14) | copy-start | bytes 12292
  14.8 9.4 %collective-permute-start = (bf16[64,128,16]{1,2,0:T(8,128)(2,1)S(1)}, bf16[64,128,16]{1,2,0:T(8,128)(2,1)S(1)}, u32[]{:S(2)}, u32[]{:S(2)}) collective-permute-start(bf16[64,128,16]{1,2,0:T(8,128)(2,1)S(1)} %copy_bitcast_fusion.2), channel_id=1, source_target_pairs={{0,4},{4,8},{8,12},{12,16},{16,20},{20,24},{24,28},{28,32},{32,36}... | collective-permute-start | bytes 786440 | tf_op jit(solution)/shard_map/ppermute | solution.py:16
  16.5 7.7 %collective-permute-start.1 = (bf16[64,128,16]{1,2,0:T(8,128)(2,1)S(1)}, bf16[64,128,16]{1,2,0:T(8,128)(2,1)S(1)}, u32[]{:S(2)}, u32[]{:S(2)}) collective-permute-start(bf16[64,128,16]{1,2,0:T(8,128)(2,1)S(1)} %copy_bitcast_fusion.2), channel_id=1, source_target_pairs={{4,0},{8,4},{12,8},{16,12},{20,16},{24,20},{28,24},{32,28},{36,32}... | collective-permute-start | bytes 786440 | tf_op jit(solution)/shard_map/ppermute | solution.py:17
  25.2 11.9 %copy-start.4 = (s32[8192]{0:T(1024)S(1)}, s32[8192]{0:T(1024)}, u32[]{:S(2)}) copy-start(s32[8192]{0:T(1024)} %param.13) | copy-start | bytes 98308
  31.0 6.1 %collective-permute-start.2 = (bf16[64,128,16]{1,2,0:T(8,128)(2,1)S(1)}, bf16[64,128,16]{1,2,0:T(8,128)(2,1)S(1)}, u32[]{:S(2)}, u32[]{:S(2)}) collective-permute-start(bf16[64,128,16]{1,2,0:T(8,128)(2,1)S(1)} %copy_bitcast_fusion.1), channel_id=1, source_target_pairs={{0,4},{4,8},{8,12},{12,16},{16,20},{20,24},{24,28},{28,32},{32,36}... | collective-permute-start | bytes 786440 | tf_op jit(solution)/shard_map/ppermute | solution.py:16
  35.7 4.7 %collective-permute-start.3 = (bf16[64,128,16]{1,2,0:T(8,128)(2,1)S(1)}, bf16[64,128,16]{1,2,0:T(8,128)(2,1)S(1)}, u32[]{:S(2)}, u32[]{:S(2)}) collective-permute-start(bf16[64,128,16]{1,2,0:T(8,128)(2,1)S(1)} %copy_bitcast_fusion.1), channel_id=1, source_target_pairs={{4,0},{8,4},{12,8},{16,12},{20,16},{24,20},{28,24},{32,28},{36,32}... | collective-permute-start | bytes 786440 | tf_op jit(solution)/shard_map/ppermute | solution.py:17
  47.0 47.3 %copy-start.1 = (bf16[8,3,128,128]{3,2,1,0:T(8,128)(2,1)S(1)}, bf16[8,3,128,128]{3,2,1,0:T(8,128)(2,1)}, u32[]{:S(2)}) copy-start(bf16[8,3,128,128]{3,2,1,0:T(8,128)(2,1)} %param.12) | copy-start | bytes 2359300
  94.6 8.6 %collective-permute-start.5 = (bf16[1,128,16]{1,2,0:T(8,128)(2,1)S(1)}, bf16[1,128,16]{1,2,0:T(8,128)(2,1)S(1)}, u32[]{:S(2)}, u32[]{:S(2)}) collective-permute-start(bf16[1,128,16]{1,2,0:T(8,128)(2,1)S(1)} %get-tuple-element.19), channel_id=1, source_target_pairs={{4,0},{8,4},{12,8},{16,12},{20,16},{24,20},{28,24},{32,28},{36,32}... | collective-permute-start | bytes 12296 | tf_op jit(solution)/shard_map/ppermute | solution.py:17
  95.9 8.1 %collective-permute-start.4 = (bf16[1,128,16]{1,2,0:T(8,128)(2,1)S(1)}, bf16[1,128,16]{1,2,0:T(8,128)(2,1)S(1)}, u32[]{:S(2)}, u32[]{:S(2)}) collective-permute-start(bf16[1,128,16]{1,2,0:T(8,128)(2,1)S(1)} %get-tuple-element.18), channel_id=1, source_target_pairs={{0,4},{4,8},{8,12},{12,16},{16,20},{20,24},{24,28},{28,32},{32,36}... | collective-permute-start | bytes 12296 | tf_op jit(solution)/shard_map/ppermute | solution.py:16
  104.5 5.5 %collective-permute-start.7 = (bf16[1,128,16]{1,2,0:T(8,128)(2,1)S(1)}, bf16[1,128,16]{1,2,0:T(8,128)(2,1)S(1)}, u32[]{:S(2)}, u32[]{:S(2)}) collective-permute-start(bf16[1,128,16]{1,2,0:T(8,128)(2,1)S(1)} %get-tuple-element.17), channel_id=1, source_target_pairs={{4,0},{8,4},{12,8},{16,12},{20,16},{24,20},{28,24},{32,28},{36,32}... | collective-permute-start | bytes 12296 | tf_op jit(solution)/shard_map/ppermute | solution.py:17
  105.8 5.0 %collective-permute-start.6 = (bf16[1,128,16]{1,2,0:T(8,128)(2,1)S(1)}, bf16[1,128,16]{1,2,0:T(8,128)(2,1)S(1)}, u32[]{:S(2)}, u32[]{:S(2)}) collective-permute-start(bf16[1,128,16]{1,2,0:T(8,128)(2,1)S(1)} %get-tuple-element.16), channel_id=1, source_target_pairs={{0,4},{4,8},{8,12},{12,16},{16,20},{20,24},{24,28},{28,32},{32,36}... | collective-permute-start | bytes 12296 | tf_op jit(solution)/shard_map/ppermute | solution.py:16
  118.6 68.6 %copy-start.2 = (f32[128,8192]{1,0:T(8,128)S(1)}, f32[128,8192]{1,0:T(8,128)}, u32[]{:S(2)}) copy-start(f32[128,8192]{1,0:T(8,128)} %param.15) | copy-start | bytes 12582916
  118.6 3.4 %collective-permute-start.8 = (f32[128,16]{1,0:T(8,128)S(1)}, f32[128,16]{1,0:T(8,128)S(1)}, u32[]{:S(2)}, u32[]{:S(2)}) collective-permute-start(f32[128,16]{1,0:T(8,128)S(1)} %slice_select_fusion), channel_id=1, source_target_pairs={{0,4},{4,0},{8,12},{12,8},{16,20},{20,16},{24,28},{28,24},{32,36},... | collective-permute-start | bytes 24584 | tf_op jit(solution)/shard_map/ppermute | solution.py:25
  193.8 1.2 collective-permute-start.9
  198.4 4.4 %collective-permute-start.11 = (bf16[1,128,16]{1,2,0:T(8,128)(2,1)S(1)}, bf16[1,128,16]{1,2,0:T(8,128)(2,1)S(1)}, u32[]{:S(2)}, u32[]{:S(2)}) collective-permute-start(bf16[1,128,16]{1,2,0:T(8,128)(2,1)S(1)} %get-tuple-element.15), channel_id=1, source_target_pairs={{4,0},{8,4},{12,8},{16,12},{20,16},{24,20},{28,24},{32,28},{36,32}... | collective-permute-start | bytes 12296 | tf_op jit(solution)/shard_map/ppermute | solution.py:17
  199.7 3.8 %collective-permute-start.10 = (bf16[1,128,16]{1,2,0:T(8,128)(2,1)S(1)}, bf16[1,128,16]{1,2,0:T(8,128)(2,1)S(1)}, u32[]{:S(2)}, u32[]{:S(2)}) collective-permute-start(bf16[1,128,16]{1,2,0:T(8,128)(2,1)S(1)} %get-tuple-element.14), channel_id=1, source_target_pairs={{0,4},{4,8},{8,12},{12,16},{16,20},{20,24},{24,28},{28,32},{32,36}... | collective-permute-start | bytes 12296 | tf_op jit(solution)/shard_map/ppermute | solution.py:16
  234.8 5.0 %collective-permute-start.12 = (bf16[64,128,16]{1,2,0:T(8,128)(2,1)S(1)}, bf16[64,128,16]{1,2,0:T(8,128)(2,1)S(1)}, u32[]{:S(2)}, u32[]{:S(2)}) collective-permute-start(bf16[64,128,16]{1,2,0:T(8,128)(2,1)S(1)} %copy_bitcast_fusion), channel_id=1, source_target_pairs={{0,4},{4,8},{8,12},{12,16},{16,20},{20,24},{24,28},{28,32},{32,36}... | collective-permute-start | bytes 786440 | tf_op jit(solution)/shard_map/ppermute | solution.py:16
  238.3 5.2 %collective-permute-start.13 = (bf16[64,128,16]{1,2,0:T(8,128)(2,1)S(1)}, bf16[64,128,16]{1,2,0:T(8,128)(2,1)S(1)}, u32[]{:S(2)}, u32[]{:S(2)}) collective-permute-start(bf16[64,128,16]{1,2,0:T(8,128)(2,1)S(1)} %copy_bitcast_fusion), channel_id=1, source_target_pairs={{4,0},{8,4},{12,8},{16,12},{20,16},{24,20},{28,24},{32,28},{36,32}... | collective-permute-start | bytes 786440 | tf_op jit(solution)/shard_map/ppermute | solution.py:17
  250.3 72.0 %copy-start.3 = (f32[8192,16]{0,1:T(8,128)}, f32[8192,16]{0,1:T(8,128)S(1)}, u32[]{:S(2)}) copy-start(f32[8192,16]{0,1:T(8,128)S(1)} %fusion.7) | copy-start | bytes 1572868
Sparse Core Ops, SparseCore 0:
  239.9 28.9 all-gather.3
